TPU v7x, 32 devices: a whole 2x2x4 slice. The times are simulated.
32 devices in a mesh: seq: 8 (over z, core), fsdp: 4 (over y, x).
Axes of the slice: x: 2, y: 2, z: 4, core: 2. Of those that a mesh axis runs over, the one named last changes fastest.
Arguments:
- layer_inputs: bfloat16 [4, 1024, 4096], P('fsdp', 'seq'), may hold values from -8 to 8
- queries: bfloat16 [4, 1024, 4096], P('fsdp', 'seq'), may hold values from -6 to 6
- key_states: bfloat16 [4, 1024, 512], P('fsdp', 'seq'), may hold values from -4 to 4
- value_states: bfloat16 [4, 1024, 512], P('fsdp', 'seq'), may hold values from -1.75 to 1.75
- output_gradient: bfloat16 [4, 1024, 4096], P('fsdp', 'seq'), may hold values from -1.75 to 1.75
- doc_blocks: int32 [4, 4], P('fsdp'), may hold values from 1 to 3, 8 in all within a row
Outputs:
- query_grad: bfloat16 [4, 1024, 4096], P('fsdp', 'seq')
- key_grad: bfloat16 [4, 1024, 512], P('fsdp', 'seq')
- value_grad: bfloat16 [4, 1024, 512], P('fsdp', 'seq')
- value_weight_grad: bfloat16 [4096, 512], P('fsdp')
Inputs may be any that keep to these rules, and one draw needn't show every extreme that they name: `doc_blocks`: the lengths of each packed row sum to 8, and each row has a document of exactly 3 blocks.
All inputs are finite; a program needn't handle non-finite values.
Results may differ from a plain program's by a relative error of at most 0.017.
Values may be sent and summed in bfloat16 or wider, within the bound.
A program may use at most 64 MiB of HBM per device.

v0:
```python
import math

import jax
import jax.numpy as jnp
from jax import lax
from jax.sharding import PartitionSpec as P

KEY_VALUE_HEADS = 4
HEAD_SIZE = 128
BLOCK = 128
QUERY_PER_KEY = 8
BACK = 2
KEYS = 384


def passed_along(x, axis, by):
    peers = lax.axis_size(axis)
    pairs = [(i, i + by) for i in range(peers) if 0 <= i + by < peers]
    return lax.ppermute(x, axis, pairs)


def document_ids(positions, doc_ends):
    block_ids = jnp.floor_divide(positions, BLOCK)
    return jnp.sum((block_ids[:, None] >= doc_ends[None, :]).astype(jnp.int32), axis=1)


def group_grads(q_group, g_group, k_group, v_group, visible, softmax_factor_scale):
    scores = (
        jnp.einsum("rhd,kd->hrk", q_group, k_group, preferred_element_type=jnp.float32)
        * softmax_factor_scale
    )
    scores = jnp.where(visible[None], scores, -jnp.inf)
    row_max = jnp.max(scores, axis=-1, keepdims=True)
    exps = jnp.exp(scores - row_max)
    probs = exps / jnp.sum(exps, axis=-1, keepdims=True)
    d_probs = jnp.einsum("rhd,kd->hrk", g_group, v_group, preferred_element_type=jnp.float32)
    deltas = jnp.sum(probs * d_probs, axis=-1, keepdims=True)
    score_gradient = (probs * (d_probs - deltas)).astype(jnp.bfloat16)
    probability_reduced = probs.astype(jnp.bfloat16)
    value_portion = jnp.einsum(
        "hrk,rhd->kd", probability_reduced, g_group, preferred_element_type=jnp.float32
    )
    key_portion = (
        jnp.einsum("hrk,rhd->kd", score_gradient, q_group, preferred_element_type=jnp.float32)
        * softmax_factor_scale
    )
    query_portion = (
        jnp.einsum("hrk,kd->rhd", score_gradient, k_group, preferred_element_type=jnp.float32)
        * softmax_factor_scale
    )
    return (query_portion, key_portion, value_portion)


def shards(layer_inputs, queries, key_states, value_states, output_gradient, doc_blocks):
    token_rows = queries.shape[1]
    my_index = lax.axis_index("seq")
    own_keys = key_states[0]
    own_values = value_states[0]
    pad_rows = BACK * token_rows
    key_blocks = []
    value_blocks = []
    for distance in range(BACK, 0, -1):
        got_keys, got_values = passed_along((own_keys, own_values), "seq", distance)
        key_blocks.append(got_keys)
        value_blocks.append(got_values)
    key_blocks.append(own_keys)
    value_blocks.append(own_values)
    window_keys = jnp.concatenate(key_blocks, axis=0)
    window_values = jnp.concatenate(value_blocks, axis=0)
    doc_ends = jnp.cumsum(doc_blocks[0])
    first_query = my_index * token_rows
    q_pos = first_query + jnp.arange(token_rows, dtype=jnp.int32)
    k_pos = first_query - pad_rows + jnp.arange(KEYS, dtype=jnp.int32)
    same_doc = document_ids(k_pos, doc_ends)[None, :] == document_ids(q_pos, doc_ends)[:, None]
    visible = same_doc & (k_pos[None, :] >= 0) & (k_pos[None, :] <= q_pos[:, None])
    softmax_factor_scale = 1.0 / math.sqrt(HEAD_SIZE)
    query_head_states = queries[0].reshape(token_rows, KEY_VALUE_HEADS, QUERY_PER_KEY, HEAD_SIZE)
    gradient_heads = output_gradient[0].reshape(
        token_rows, KEY_VALUE_HEADS, QUERY_PER_KEY, HEAD_SIZE
    )
    query_portions = []
    key_parts = []
    value_parts = []
    for key_value_group in range(KEY_VALUE_HEADS):
        k_group = window_keys[:, key_value_group * HEAD_SIZE : (key_value_group + 1) * HEAD_SIZE]
        v_group = window_values[:, key_value_group * HEAD_SIZE : (key_value_group + 1) * HEAD_SIZE]
        query_portion, key_portion, value_portion = group_grads(
            query_head_states[:, key_value_group],
            gradient_heads[:, key_value_group],
            k_group,
            v_group,
            visible,
            softmax_factor_scale,
        )
        query_portions.append(query_portion)
        key_parts.append(key_portion)
        value_parts.append(value_portion)
    query_grad = (
        jnp.stack(query_portions, axis=1)
        .reshape(token_rows, KEY_VALUE_HEADS * QUERY_PER_KEY * HEAD_SIZE)
        .astype(jnp.bfloat16)
    )
    key_window = jnp.concatenate(key_parts, axis=1)
    value_window = jnp.concatenate(value_parts, axis=1)
    key_total = key_window[pad_rows:]
    value_total = value_window[pad_rows:]
    for distance in range(1, BACK + 1):
        lower = (BACK - distance) * token_rows
        got_keys, got_values = (
            passed_along(
                key_window[lower : lower + token_rows].astype(jnp.bfloat16), "seq", -distance
            ).astype(jnp.float32),
            passed_along(
                value_window[lower : lower + token_rows].astype(jnp.bfloat16), "seq", -distance
            ).astype(jnp.float32),
        )
        key_total = key_total + got_keys
        value_total = value_total + got_values
    key_grad = key_total.astype(jnp.bfloat16)
    value_grad = value_total.astype(jnp.bfloat16)
    local_inputs = layer_inputs[0]
    weight_share = lax.psum_scatter(
        lax.dot_general(
            local_inputs, value_grad, (((0,), (0,)), ((), ())), preferred_element_type=jnp.float32
        ).astype(jnp.bfloat16),
        "fsdp",
        scatter_dimension=0,
        tiled=True,
    )
    weight_total = lax.psum(weight_share, "seq").astype(jnp.float32)
    token_count = lax.axis_size("fsdp") * lax.axis_size("seq") * token_rows
    value_weight_grad = (weight_total / math.sqrt(token_count)).astype(jnp.bfloat16)
    return (query_grad[None], key_grad[None], value_grad[None], value_weight_grad)


def solution(mesh):
    placed = (
        P("fsdp", "seq", None),
        P("fsdp", "seq", None),
        P("fsdp", "seq", None),
        P("fsdp", "seq", None),
        P("fsdp", "seq", None),
        P("fsdp", None),
    )
    return jax.shard_map(
        shards,
        mesh=mesh,
        in_specs=placed,
        out_specs=(
            P("fsdp", "seq", None),
            P("fsdp", "seq", None),
            P("fsdp", "seq", None),
            P("fsdp", None),
        ),
        check_vma=False,
    )
```

profile of v0, /device:TPU:0, one launch (start us, length us, event | category | flops | bytes accessed | tf_op | source)
XLA Modules:
  0.0 170.2 jit_solution(6440243550890889599)
XLA Ops:
  7.2 2.5 %collective-permute-start.1 = (bf16[128,512]{1,0:T(8,128)(2,1)}, bf16[128,512]{1,0:T(8,128)(2,1)S(1)}, u32[]{:S(2)}, u32[]{:S(2)}) collective-permute-start(bf16[128,512]{1,0:T(8,128)(2,1)} %bitcast.294), channel_id=1, source_target_pairs={{0,4},{4,8},{8,12},{12,16},{16,20},{20,24},{24,28},{1,5},{5,9},{9,... | collective-permute-start | bytes 393224 | tf_op jit(solution)/shard_map/ppermute | solution.py:19
  9.8 4.5 %collective-permute-start = (bf16[128,512]{1,0:T(8,128)(2,1)}, bf16[128,512]{1,0:T(8,128)(2,1)S(1)}, u32[]{:S(2)}, u32[]{:S(2)}) collective-permute-start(bf16[128,512]{1,0:T(8,128)(2,1)} %bitcast.295), channel_id=1, source_target_pairs={{0,8},{4,12},{8,16},{12,20},{16,24},{20,28},{1,9},{5,13},{9,17},{1... | collective-permute-start | bytes 393224 | tf_op jit(solution)/shard_map/ppermute | solution.py:19
  15.9 1.6 copy.76
  17.5 1.3 copy.78
  19.8 1.8 %fusion.72 = (f32[8,128]{1,0:T(8,128)S(1)}, f32[8,128,384]{1,2,0:T(8,128)}) fusion(pred[128,384]{0,1:T(8,128)(4,1)S(1)} %compare_and_fusion, bf16[128,4,8,128]{0,3,2,1:T(8,128)(2,1)S(1)} %bitcast.276, bf16[384,512]{1,0:T(8,128)(2,1)S(1)} %pad_maximum_fusion.3), kind=kOutput, calls=%fused_computation.139 | convolution fusion | flops 102236544 | bytes 1986560 | tf_op jit(solution)/shard_map/sub | solution.py:34
  21.6 1.8 %fusion.73 = (f32[8,128]{1,0:T(8,128)S(1)}, f32[8,128,384]{1,2,0:T(8,128)}) fusion(pred[128,384]{0,1:T(8,128)(4,1)S(1)} %compare_and_fusion, bf16[128,4,8,128]{0,3,2,1:T(8,128)(2,1)S(1)} %bitcast.277, bf16[384,512]{1,0:T(8,128)(2,1)S(1)} %pad_maximum_fusion.3), kind=kOutput, calls=%fused_computation.140 | convolution fusion | flops 102236544 | bytes 1986560 | tf_op jit(solution)/shard_map/sub | solution.py:34
  23.4 1.8 %fusion.74 = (f32[8,128]{1,0:T(8,128)S(1)}, f32[8,128,384]{1,2,0:T(8,128)}) fusion(pred[128,384]{0,1:T(8,128)(4,1)S(1)} %compare_and_fusion, bf16[128,4,8,128]{0,3,2,1:T(8,128)(2,1)S(1)} %bitcast.278, bf16[384,512]{1,0:T(8,128)(2,1)S(1)} %pad_maximum_fusion.3), kind=kOutput, calls=%fused_computation.141 | convolution fusion | flops 102236544 | bytes 1986560 | tf_op jit(solution)/shard_map/sub | solution.py:34
  25.1 1.8 %fusion.71 = (f32[8,128]{1,0:T(8,128)S(1)}, f32[8,128,384]{1,2,0:T(8,128)}) fusion(pred[128,384]{0,1:T(8,128)(4,1)S(1)} %compare_and_fusion, bf16[128,4,8,128]{0,3,2,1:T(8,128)(2,1)S(1)} %bitcast.279, bf16[384,512]{1,0:T(8,128)(2,1)S(1)} %pad_maximum_fusion.3), kind=kOutput, calls=%fused_computation.138 | convolution fusion | flops 102236544 | bytes 1986560 | tf_op jit(solution)/shard_map/sub | solution.py:34
  26.9 1.9 %convolution_bitcast_fusion.1 = f32[384,128]{0,1:T(8,128)S(1)} fusion(bf16[128,4,8,128]{0,3,2,1:T(8,128)(2,1)} %bitcast.286, f32[8,128,384]{1,2,0:T(8,128)} %get-tuple-element.25, f32[8,128]{1,0:T(8,128)S(1)} %get-tuple-element.24), kind=kOutput, calls=%fused_computation.52 | convolution fusion | flops 101449728 | bytes 2035712 | tf_op jit(solution)/shard_map/hrk,rhd->kd/dot_general | solution.py:40
  35.1 1.5 collective-permute-done.6
  36.6 6.5 %collective-permute-done.7 = bf16[128,512]{0,1:T(8,128)(2,1)S(1)} collective-permute-done((bf16[128,512]{0,1:T(8,128)(2,1)S(1)}, bf16[128,512]{0,1:T(8,128)(2,1)S(1)}, u32[]{:S(2)}, u32[]{:S(2)}) %collective-permute-start.7) | collective-permute-done | bytes 131104 | tf_op jit(solution)/shard_map/ppermute | solution.py:19
  43.2 3.2 %fusion.4 = bf16[4096,512]{0,1:T(8,128)(2,1)} fusion(bf16[128,512]{0,1:T(8,128)(2,1)S(1)} %fusion.43, bf16[1,128,4096]{2,1,0:T(8,128)(2,1)S(1)} %copy-done), kind=kOutput, calls=%fused_computation.5 | convolution fusion | flops 538968064 | bytes 5373952 | tf_op jit(solution)/shard_map/dot_general | solution.py:123
  47.3 1.5 collective-permute-start.3
  48.8 3.9 %collective-permute-start.2 = (bf16[128,512]{1,0:T(8,128)(2,1)S(1)}, bf16[128,512]{1,0:T(8,128)(2,1)S(1)}, u32[]{:S(2)}, u32[]{:S(2)}) collective-permute-start(bf16[128,512]{1,0:T(8,128)(2,1)S(1)} %bitcast.298), channel_id=1, source_target_pairs={{0,8},{4,12},{8,16},{12,20},{16,24},{20,28},{1,9},{5,13},{9,17},{1... | collective-permute-start | bytes 393224 | tf_op jit(solution)/shard_map/ppermute | solution.py:19
  52.7 3.6 %collective-permute-done.2 = bf16[128,512]{1,0:T(8,128)(2,1)S(1)} collective-permute-done((bf16[128,512]{1,0:T(8,128)(2,1)S(1)}, bf16[128,512]{1,0:T(8,128)(2,1)S(1)}, u32[]{:S(2)}, u32[]{:S(2)}) %collective-permute-start.2) | collective-permute-done | bytes 131104 | tf_op jit(solution)/shard_map/ppermute | solution.py:19
  56.3 1.4 fusion.12
  65.4 2.3 %copy.110 = bf16[1,128,4096]{2,1,0:T(8,128)(2,1)} copy(bf16[1,128,4096]{1,2,0:T(8,128)(2,1)} %bitcast.284) | data formatting | bytes 2097152
  67.7 1.5 fusion.34
  69.2 1.4 fusion.35
  71.4 27.5 %reduce-scatter.2.cloned.1.call-done = bf16[1024,512]{0,1:T(8,128)(2,1)} async-done(((bf16[4096,512]{0,1:T(8,128)(2,1)}), bf16[1024,512]{0,1:T(8,128)(2,1)}) %reduce-scatter.2.cloned.1.call-update) | async-done | bytes 1048592 | tf_op jit(solution)/shard_map/reduce_scatter | solution.py:122
  102.5 6.2 %collective-permute-done.5 = bf16[128,512]{0,1:T(8,128)(2,1)S(1)} collective-permute-done((bf16[128,512]{0,1:T(8,128)(2,1)S(1)}, bf16[128,512]{0,1:T(8,128)(2,1)S(1)}, u32[]{:S(2)}, u32[]{:S(2)}) %collective-permute-start.5) | collective-permute-done | bytes 131104 | tf_op jit(solution)/shard_map/ppermute | solution.py:19
  109.4 51.2 %all-reduce.2.cloned.1.call-done = bf16[1024,512]{0,1:T(8,128)(2,1)} async-done(((bf16[1024,512]{0,1:T(8,128)(2,1)}), bf16[1024,512]{0,1:T(8,128)(2,1)}) %all-reduce.2.cloned.1.call-update) | async-done | bytes 1048592 | tf_op jit(solution)/shard_map/psum | solution.py:130
  160.6 1.4 multiply_convert_fusion
  162.0 1.3 copy.113
  (94 shorter events, 22.2 us)
Async XLA Ops:
  7.2 36.0 %copy-start = (bf16[1,128,4096]{2,1,0:T(8,128)(2,1)S(1)}, bf16[1,128,4096]{2,1,0:T(8,128)(2,1)}, u32[]{:S(2)}) copy-start(bf16[1,128,4096]{2,1,0:T(8,128)(2,1)} %param.6) | copy-start | bytes 3145732
  7.2 10.3 %copy-start.17 = (bf16[1,128,4096]{2,1,0:T(8,128)(2,1)S(1)}, bf16[1,128,4096]{2,1,0:T(8,128)(2,1)}, u32[]{:S(2)}) copy-start(bf16[1,128,4096]{2,1,0:T(8,128)(2,1)} %param.10) | copy-start | bytes 3145732
  7.2 91.8 %reduce-scatter.2.cloned.1.call-start = ((), (), s32[]{:S(2)}) async-start(), calls=%async_computation.1 | async-start | bytes 5242880 | tf_op jit(solution)/shard_map/reduce_scatter | solution.py:122
  7.2 12.5 %collective-permute-start.1 = (bf16[128,512]{1,0:T(8,128)(2,1)}, bf16[128,512]{1,0:T(8,128)(2,1)S(1)}, u32[]{:S(2)}, u32[]{:S(2)}) collective-permute-start(bf16[128,512]{1,0:T(8,128)(2,1)} %bitcast.294), channel_id=1, source_target_pairs={{0,4},{4,8},{8,12},{12,16},{16,20},{20,24},{24,28},{1,5},{5,9},{9,... | collective-permute-start | bytes 393224 | tf_op jit(solution)/shard_map/ppermute | solution.py:19
  9.8 9.9 %collective-permute-start = (bf16[128,512]{1,0:T(8,128)(2,1)}, bf16[128,512]{1,0:T(8,128)(2,1)S(1)}, u32[]{:S(2)}, u32[]{:S(2)}) collective-permute-start(bf16[128,512]{1,0:T(8,128)(2,1)} %bitcast.295), channel_id=1, source_target_pairs={{0,8},{4,12},{8,16},{12,20},{16,24},{20,28},{1,9},{5,13},{9,17},{1... | collective-permute-start | bytes 393224 | tf_op jit(solution)/shard_map/ppermute | solution.py:19
  17.5 7.7 %copy-start.3 = (bf16[1,128,4096]{1,2,0:T(8,128)(2,1)}, bf16[1,128,4096]{1,2,0:T(8,128)(2,1)S(1)}, u32[]{:S(2)}) copy-start(bf16[1,128,4096]{1,2,0:T(8,128)(2,1)S(1)} %copy.76) | copy-start | bytes 3145732
  17.5 2.2 %copy-start.20 = (bf16[1,128,512]{2,1,0:T(8,128)(2,1)S(1)}, bf16[1,128,512]{2,1,0:T(8,128)(2,1)}, u32[]{:S(2)}) copy-start(bf16[1,128,512]{2,1,0:T(8,128)(2,1)} %param.8) | copy-start | bytes 393220
  19.8 40.3 %copy-start.7 = (bf16[384,512]{1,0:T(8,128)(2,1)}, bf16[384,512]{1,0:T(8,128)(2,1)S(1)}, u32[]{:S(2)}) copy-start(bf16[384,512]{1,0:T(8,128)(2,1)S(1)} %pad_maximum_fusion.3) | copy-start | bytes 1179652
  26.9 2.0 %copy-start.13 = (f32[8,128,384]{1,2,0:T(8,128)S(1)}, f32[8,128,384]{1,2,0:T(8,128)}, u32[]{:S(2)}) copy-start(f32[8,128,384]{1,2,0:T(8,128)} %get-tuple-element.29) | copy-start | bytes 4718596
  26.9 2.2 %copy-start.18 = (bf16[1,128,4096]{1,2,0:T(8,128)(2,1)S(1)}, bf16[1,128,4096]{1,2,0:T(8,128)(2,1)}, u32[]{:S(2)}) copy-start(bf16[1,128,4096]{1,2,0:T(8,128)(2,1)} %copy.78) | copy-start | bytes 3145732
  32.5 4.1 %collective-permute-start.6 = (bf16[128,512]{0,1:T(8,128)(2,1)S(1)}, bf16[128,512]{0,1:T(8,128)(2,1)S(1)}, u32[]{:S(2)}, u32[]{:S(2)}) collective-permute-start(bf16[128,512]{0,1:T(8,128)(2,1)S(1)} %get-tuple-element.16), channel_id=1, source_target_pairs={{4,0},{8,4},{12,8},{16,12},{20,16},{24,20},{28,24},{5,1},{9,5},{13... | collective-permute-start | bytes 393224 | tf_op jit(solution)/shard_map/ppermute | solution.py:19
  33.8 9.4 %collective-permute-start.7 = (bf16[128,512]{0,1:T(8,128)(2,1)S(1)}, bf16[128,512]{0,1:T(8,128)(2,1)S(1)}, u32[]{:S(2)}, u32[]{:S(2)}) collective-permute-start(bf16[128,512]{0,1:T(8,128)(2,1)S(1)} %get-tuple-element.17), channel_id=1, source_target_pairs={{8,0},{12,4},{16,8},{20,12},{24,16},{28,20},{9,1},{13,5},{17,9},{2... | collective-permute-start | bytes 393224 | tf_op jit(solution)/shard_map/ppermute | solution.py:19
  46.4 9.9 %copy-start.15 = (f32[8,128,384]{1,2,0:T(8,128)S(1)}, f32[8,128,384]{1,2,0:T(8,128)}, u32[]{:S(2)}) copy-start(f32[8,128,384]{1,2,0:T(8,128)} %get-tuple-element.25) | copy-start | bytes 4718596
  46.4 114.2 %all-reduce.2.cloned.1.call-start = ((), (), s32[]{:S(2)}) async-start(), calls=%async_computation.2 | async-start | bytes 2097152 | tf_op jit(solution)/shard_map/psum | solution.py:130
  47.3 5.4 %collective-permute-start.3 = (bf16[128,512]{1,0:T(8,128)(2,1)S(1)}, bf16[128,512]{1,0:T(8,128)(2,1)S(1)}, u32[]{:S(2)}, u32[]{:S(2)}) collective-permute-start(bf16[128,512]{1,0:T(8,128)(2,1)S(1)} %bitcast.297), channel_id=1, source_target_pairs={{0,4},{4,8},{8,12},{12,16},{16,20},{20,24},{24,28},{1,5},{5,9},{9,... | collective-permute-start | bytes 393224 | tf_op jit(solution)/shard_map/ppermute | solution.py:19
  48.8 7.5 %collective-permute-start.2 = (bf16[128,512]{1,0:T(8,128)(2,1)S(1)}, bf16[128,512]{1,0:T(8,128)(2,1)S(1)}, u32[]{:S(2)}, u32[]{:S(2)}) collective-permute-start(bf16[128,512]{1,0:T(8,128)(2,1)S(1)} %bitcast.298), channel_id=1, source_target_pairs={{0,8},{4,12},{8,16},{12,20},{16,24},{20,28},{1,9},{5,13},{9,17},{1... | collective-permute-start | bytes 393224 | tf_op jit(solution)/shard_map/ppermute | solution.py:19
  57.8 1.7 copy-start.19
  61.6 1.7 %copy-start.10 = (f32[8,128,384]{1,2,0:T(8,128)S(1)}, f32[8,128,384]{1,2,0:T(8,128)}, u32[]{:S(2)}) copy-start(f32[8,128,384]{1,2,0:T(8,128)} %get-tuple-element.33) | copy-start | bytes 4718596
  67.7 2.9 %copy-start.2 = (bf16[8,128,384]{1,2,0:T(8,128)(2,1)S(1)}, bf16[8,128,384]{1,2,0:T(8,128)(2,1)}, u32[]{:S(2)}) copy-start(bf16[8,128,384]{1,2,0:T(8,128)(2,1)} %copy-done.1) | copy-start | bytes 2359300
  67.7 2.9 %copy-start.4 = (bf16[1,128,4096]{1,2,0:T(8,128)(2,1)S(1)}, bf16[1,128,4096]{1,2,0:T(8,128)(2,1)}, u32[]{:S(2)}) copy-start(bf16[1,128,4096]{1,2,0:T(8,128)(2,1)} %copy-done.3) | copy-start | bytes 3145732
  69.2 2.2 %copy-start.5 = (f32[384,128]{0,1:T(8,128)}, f32[384,128]{0,1:T(8,128)S(1)}, u32[]{:S(2)}) copy-start(f32[384,128]{0,1:T(8,128)S(1)} %fusion.34) | copy-start | bytes 589828
  71.4 30.2 %copy-start.6 = (f32[384,128]{0,1:T(8,128)S(1)}, f32[384,128]{0,1:T(8,128)}, u32[]{:S(2)}) copy-start(f32[384,128]{0,1:T(8,128)} %copy-done.5) | copy-start | bytes 589828
  99.0 3.4 %collective-permute-start.4 = (bf16[128,512]{0,1:T(8,128)(2,1)S(1)}, bf16[128,512]{0,1:T(8,128)(2,1)S(1)}, u32[]{:S(2)}, u32[]{:S(2)}) collective-permute-start(bf16[128,512]{0,1:T(8,128)(2,1)S(1)} %get-tuple-element.18), channel_id=1, source_target_pairs={{4,0},{8,4},{12,8},{16,12},{20,16},{24,20},{28,24},{5,1},{9,5},{13... | collective-permute-start | bytes 393224 | tf_op jit(solution)/shard_map/ppermute | solution.py:19
  100.3 8.3 %collective-permute-start.5 = (bf16[128,512]{0,1:T(8,128)(2,1)S(1)}, bf16[128,512]{0,1:T(8,128)(2,1)S(1)}, u32[]{:S(2)}, u32[]{:S(2)}) collective-permute-start(bf16[128,512]{0,1:T(8,128)(2,1)S(1)} %get-tuple-element.19), channel_id=1, source_target_pairs={{8,0},{12,4},{16,8},{20,12},{24,16},{28,20},{9,1},{13,5},{17,9},{2... | collective-permute-start | bytes 393224 | tf_op jit(solution)/shard_map/ppermute | solution.py:19
  (8 other events, 10.5 us)
Sparse Core Ops, SparseCore 0:
  46.5 52.3 reduce-scatter.1
  101.3 59.2 all-reduce.1
where the time goes:
time: 171 us; the launch traced here: 170 us
  waiting for transfers between devices  96.5 us (56%)
  matrix products  20.8 us (12%)
  starting transfers between devices  17.7 us (10%)
  between operations  14.6 us (9%)
  local copies, waits for them, and re-layouts  14.5 us (8%)
  other arithmetic  6.15 us (4%)
    psum x1, waiting for transfers between devices, shards(): weight_total = lax.psum(weight_share, 'seq').astype(jnp.float32)  51.2 us
    reduce_scatter x1, waiting for transfers between devices, shards(): lax.psum_scatter(lax.dot_general(local_inputs, value_grad, (((0,), (0,)),...  27.5 us
    ppermute x8, waiting for transfers between devices, passed_along(): return lax.ppermute(x, axis, pairs)  17.8 us
    ppermute x8, starting transfers between devices, passed_along(): return lax.ppermute(x, axis, pairs)  17.6 us
    unnamed x50, local copies, waits for them, and re-layouts  14.5 us
    sub x4, matrix products, group_grads(): exps = jnp.exp(scores - row_max)  7.15 us
    dot_general x4, matrix products, group_grads(): jnp.einsum('hrk,rhd->kd', score_gradient, q_group, preferred_element_type...  3.6 us
  transfers between devices with their start and end apart: 10, of which 6 were waited for; matrix products, arithmetic and copies ran while one was open for 11% of the time, Pallas kernels for 0%

commit v1 on v0

v1 whole, which is shorter than its diff:
```python
import functools
import math

import jax
import jax.numpy as jnp
from jax import lax
from jax.experimental import pallas as pl
from jax.experimental.pallas import tpu as pltpu
from jax.sharding import PartitionSpec as P

HEAD_SIZE = 128
BLOCK = 128
BACK = 2
PAIR = 2
HALVES = 2
SUB = 4
MESH = pl.DeviceIdType.MESH
F32 = jnp.float32
BF16 = jnp.bfloat16


def matmul(a, b, ca, cb):
    return lax.dot_general(a, b, (((ca,), (cb,)), ((), ())), preferred_element_type=F32)


def kernel(
    n_s, n_f, groups, heads,
    doc_ref, x_hbm, q_hbm, k_hbm, v_hbm, g_hbm,
    dq_out, dk_out, vg_out, w_out,
    q, g, kwin, vwin, xg, probs, bias, dq,
    dv_own, dv_send, dv_recv, dk_own, dk_send, dk_recv, dkb, vgb,
    w_own, pair_send, pair_recv, right_send, left_recv, left_send, right_recv, wfin,
    loc_sem, out_sem, k_ss, k_rs, v_ss, v_rs, x_ss, x_rs,
    dv_ss, dv_rs, dk_ss, dk_rs, vg_ss, vg_rs, p_ss, p_rs,
    r_ss, r_rs, l_ss, l_rs, f_ss, f_rs,
):
    s = lax.axis_index("seq")
    f = lax.axis_index("fsdp")
    rows = q.shape[0]
    width = xg.shape[2]
    kvw = groups * HEAD_SIZE
    keys = (BACK + 1) * rows
    chunks = HALVES * SUB
    half_cols = kvw // HALVES
    half_rows = width // 2
    sub_rows = half_rows // SUB
    core = s % 2
    z = s // 2
    depth = n_s // 2
    sibling = s + 1 - 2 * core
    scale = 1.0 / math.sqrt(HEAD_SIZE)

    def remote(src, dst, ss, rs, to_s, to_f):
        return pltpu.make_async_remote_copy(
            src_ref=src, dst_ref=dst, send_sem=ss, recv_sem=rs,
            device_id={"seq": to_s, "fsdp": to_f}, device_id_type=MESH,
        )

    local = [
        pltpu.make_async_copy(q_hbm.at[0], q, loc_sem.at[0]),
        pltpu.make_async_copy(g_hbm.at[0], g, loc_sem.at[1]),
        pltpu.make_async_copy(k_hbm.at[0], kwin.at[BACK], loc_sem.at[2]),
        pltpu.make_async_copy(v_hbm.at[0], vwin.at[BACK], loc_sem.at[3]),
        pltpu.make_async_copy(
            x_hbm.at[0, :, pl.ds(pl.multiple_of(f * width, 128), width)], xg.at[f], loc_sem.at[4]
        ),
    ]
    for copy in local:
        copy.start()

    barrier = pltpu.get_barrier_semaphore()
    for d in range(1, BACK + 1):
        @pl.when(s >= d)
        def _():
            pl.semaphore_signal(
                barrier, inc=1, device_id={"seq": s - d, "fsdp": f}, device_id_type=MESH
            )

        @pl.when(s + d < n_s)
        def _():
            pl.semaphore_signal(
                barrier, inc=1, device_id={"seq": s + d, "fsdp": f}, device_id_type=MESH
            )
    for j in range(1, n_f):
        pl.semaphore_signal(
            barrier, inc=1, device_id={"seq": s, "fsdp": (f + j) % n_f}, device_id_type=MESH
        )

    def doc_of(block):
        end = jnp.int32(0)
        doc = jnp.int32(0)
        for i in range(doc_ref.shape[1]):
            end = end + doc_ref[0, i]
            doc = doc + jnp.where(block >= end, 1, 0)
        return doc

    mine = doc_of(s)
    for d in range(1, BACK + 1):
        seen = jnp.logical_and(doc_of(s - d) == mine, s >= d)
        level = jnp.where(seen, 0.0, -jnp.inf).astype(F32)
        bias[(BACK - d) * rows : (BACK - d + 1) * rows, :] = jnp.full(
            (rows, PAIR * rows), level, F32
        )
    key_at = lax.broadcasted_iota(jnp.int32, (rows, PAIR * rows), 0)
    query_at = lax.broadcasted_iota(jnp.int32, (rows, PAIR * rows), 1) % rows
    bias[BACK * rows :, :] = jnp.where(key_at <= query_at, 0.0, -jnp.inf).astype(F32)

    for d in range(1, BACK + 1):
        @pl.when(s < d)
        def _():
            kwin[BACK - d] = jnp.zeros((rows, kvw), BF16)
            vwin[BACK - d] = jnp.zeros((rows, kvw), BF16)

        @pl.when(s + d >= n_s)
        def _():
            dv_recv[d - 1] = jnp.zeros((rows, kvw), BF16)
            dk_recv[d - 1] = jnp.zeros((rows, kvw), BF16)

    @pl.when(z == 0)
    def _():
        left_recv[...] = jnp.zeros_like(left_recv)

    @pl.when(z == depth - 1)
    def _():
        right_recv[...] = jnp.zeros_like(right_recv)

    one = lambda c: jnp.where(c, 1, 0)
    pl.semaphore_wait(
        barrier, n_f - 1 + one(s >= 1) + one(s >= 2) + one(s + 1 < n_s) + one(s + 2 < n_s)
    )

    def group_cols(i):
        return pl.ds(pl.multiple_of(i * HEAD_SIZE, HEAD_SIZE), HEAD_SIZE)

    def k_copy(d, i):
        return remote(
            k_hbm.at[0, :, group_cols(i)], kwin.at[BACK - d, :, group_cols(i)],
            k_ss.at[d - 1, i], k_rs.at[d - 1, i], s + d, f,
        )

    def v_copy(d):
        return remote(
            v_hbm.at[0], vwin.at[BACK - d], v_ss.at[d - 1], v_rs.at[d - 1], s + d, f
        )

    def x_copy(j):
        to = (f + j) % n_f
        return remote(
            x_hbm.at[0, :, pl.ds(pl.multiple_of(to * width, 128), width)], xg.at[f],
            x_ss.at[j], x_rs.at[j], s, to,
        )

    for i in range(groups):
        for d in range(1, BACK + 1):
            @pl.when(s + d < n_s)
            def _():
                k_copy(d, i).start()
    for d in range(1, BACK + 1):
        @pl.when(s + d < n_s)
        def _():
            v_copy(d).start()
    for j in range(1, n_f):
        x_copy(j).start()

    for copy in local[:3]:
        copy.wait()

    def back_copy(send, recv, ss, rs, d, i):
        return remote(
            send.at[d - 1, :, group_cols(i)], recv.at[d - 1, :, group_cols(i)],
            ss.at[d - 1, i], rs.at[d - 1, i], s - d, f,
        )

    def pair_of(ref, i, j):
        first = (i * heads + j * PAIR) * HEAD_SIZE
        return jnp.concatenate(
            [
                ref[:, pl.ds(pl.multiple_of(first + n * HEAD_SIZE, HEAD_SIZE), HEAD_SIZE)]
                for n in range(PAIR)
            ],
            axis=0,
        )

    def give_back(total, own, send, recv, ss, rs, i):
        own[:, group_cols(i)] = total[BACK * rows :]
        for d in range(1, BACK + 1):
            send[d - 1, :, group_cols(i)] = total[(BACK - d) * rows : (BACK - d + 1) * rows].astype(
                BF16
            )

            @pl.when(s >= d)
            def _():
                back_copy(send, recv, ss, rs, d, i).start()

    def first_pass(i, carry):
        for d in range(1, BACK + 1):
            @pl.when(s >= d)
            def _():
                k_copy(d, i).wait_recv()
        k_group = kwin[:, :, group_cols(i)].reshape(keys, HEAD_SIZE)
        total = jnp.zeros((keys, HEAD_SIZE), F32)
        for j in range(heads // PAIR):
            scores = matmul(k_group, pair_of(q, i, j), 1, 1)
            scores = scores * (scale * math.log2(math.e)) + bias[...]
            exps = jnp.exp2(scores - jnp.max(scores, axis=0, keepdims=True))
            p = exps * (1.0 / jnp.sum(exps, axis=0, keepdims=True))
            probs[i, j] = p
            total = total + matmul(p.astype(BF16), pair_of(g, i, j), 1, 0)
        give_back(total, dv_own, dv_send, dv_recv, dv_ss, dv_rs, i)
        return carry

    lax.fori_loop(0, groups, first_pass, 0)

    local[3].wait()
    for d in range(1, BACK + 1):
        @pl.when(s >= d)
        def _():
            v_copy(d).wait_recv()

    def second_pass(i, carry):
        k_group = kwin[:, :, group_cols(i)].reshape(keys, HEAD_SIZE)
        v_group = vwin[:, :, group_cols(i)].reshape(keys, HEAD_SIZE)
        k_turned = k_group.T
        total = jnp.zeros((keys, HEAD_SIZE), F32)
        for j in range(heads // PAIR):
            p = probs[i, j]
            d_probs = matmul(v_group, pair_of(g, i, j), 1, 1)
            deltas = jnp.sum(p * d_probs, axis=0, keepdims=True)
            d_scores = (p * (d_probs - deltas)).astype(BF16)
            total = total + matmul(d_scores, pair_of(q, i, j), 1, 0)
            turned = (matmul(k_turned, d_scores, 1, 0) * scale).T.astype(BF16)
            first = (i * heads + j * PAIR) * HEAD_SIZE
            for n in range(PAIR):
                cols = pl.ds(pl.multiple_of(first + n * HEAD_SIZE, HEAD_SIZE), HEAD_SIZE)
                dq[:, cols] = turned[n * rows : (n + 1) * rows]
        give_back(total * scale, dk_own, dk_send, dk_recv, dk_ss, dk_rs, i)
        return carry

    def vg_copy(h, j):
        cols = pl.ds(h * half_cols, half_cols)
        return remote(
            vgb.at[f, :, cols], vgb.at[f, :, cols], vg_ss.at[h, j], vg_rs.at[h, j],
            s, (f + j) % n_f,
        )

    per_half = groups // HALVES

    def collect(own, recv, send, ss, rs, lo, count):
        for i in range(lo, lo + count):
            for d in range(1, BACK + 1):
                @pl.when(s + d < n_s)
                def _():
                    back_copy(send, recv, ss, rs, d, i).wait_recv()
        cols = slice(lo * HEAD_SIZE, (lo + count) * HEAD_SIZE)
        total = own[:, cols]
        for d in range(1, BACK + 1):
            total = total + recv[d - 1, :, cols].astype(F32)
        return total.astype(BF16)

    def value_half(h):
        cols = slice(h * half_cols, (h + 1) * half_cols)
        vgb[f, :, cols] = collect(dv_own, dv_recv, dv_send, dv_ss, dv_rs, h * per_half, per_half)
        for j in range(1, n_f):
            vg_copy(h, j).start()

    def pair_copy(h):
        return remote(
            pair_send.at[h], pair_recv.at[h], p_ss.at[h], p_rs.at[h], sibling, f
        )

    def weight_half(h):
        for j in range(1, n_f):
            vg_copy(h, j).wait_recv()
        values = vgb[:, :, h * half_cols : (h + 1) * half_cols].reshape(n_f * rows, half_cols)

        def part(which):
            lhs = xg[:, :, pl.ds(pl.multiple_of(which * half_rows, half_rows), half_rows)]
            return matmul(lhs.reshape(n_f * rows, half_rows), values, 0, 0)

        pair_send[h] = part(1 - core).astype(BF16)
        pair_copy(h).start()
        w_own[h] = part(core)

    lax.fori_loop(0, 1, second_pass, 0)
    value_half(0)
    lax.fori_loop(1, 3, second_pass, 0) if groups > 3 else None
    value_half(1)
    lax.fori_loop(3 if groups > 3 else 1, groups, second_pass, 0)
    dq_copy = pltpu.make_async_copy(dq, dq_out.at[0], out_sem.at[0])
    dq_copy.start()
    vg_save = pltpu.make_async_copy(vgb.at[f], vg_out.at[0], out_sem.at[1])
    vg_save.start()
    local[4].wait()
    for j in range(1, n_f):
        x_copy(j).wait_recv()
    for h in range(HALVES):
        weight_half(h)
    for h in range(HALVES):
        pair_copy(h).wait_recv()
        w_own[h] = w_own[h] + pair_recv[h].astype(F32)

    def right_copy(c):
        return remote(right_send.at[c], left_recv.at[c], r_ss.at[c], r_rs.at[c], s + 2, f)

    def left_copy(c):
        return remote(left_send.at[c], right_recv.at[c], l_ss.at[c], l_rs.at[c], s - 2, f)

    def place(c, side):
        at = side * half_rows + (c % SUB) * sub_rows
        return wfin.at[
            pl.ds(pl.multiple_of(at, sub_rows), sub_rows),
            pl.ds(pl.multiple_of((c // SUB) * half_cols, half_cols), half_cols),
        ]

    def final_copy(c):
        return remote(place(c, core), place(c, core), f_ss.at[c], f_rs.at[c], sibling, f)

    def own_chunk(c):
        return w_own[c // SUB, pl.ds(pl.multiple_of((c % SUB) * sub_rows, sub_rows), sub_rows), :]

    token_count = n_f * n_s * rows

    def step(t, carry):
        to_right = t - z
        to_left = t - (depth - 1 - z)
        done = t - jnp.maximum(z, depth - 1 - z)

        def inside(c):
            return jnp.logical_and(c >= 0, c < chunks)

        @pl.when(jnp.logical_and(inside(to_right), z > 0))
        def _():
            right_copy(to_right).wait_recv()

        @pl.when(jnp.logical_and(inside(to_right), z < depth - 1))
        def _():
            right_send[to_right] = (own_chunk(to_right) + left_recv[to_right].astype(F32)).astype(
                BF16
            )
            right_copy(to_right).start()

        @pl.when(jnp.logical_and(inside(to_left), z < depth - 1))
        def _():
            left_copy(to_left).wait_recv()

        @pl.when(jnp.logical_and(inside(to_left), z > 0))
        def _():
            left_send[to_left] = (own_chunk(to_left) + right_recv[to_left].astype(F32)).astype(BF16)
            left_copy(to_left).start()

        @pl.when(inside(done))
        def _():
            total = own_chunk(done) + left_recv[done].astype(F32) + right_recv[done].astype(F32)
            place(done, core)[...] = (total * (1.0 / math.sqrt(token_count))).astype(BF16)
            final_copy(done).start()

        return carry

    lax.fori_loop(0, chunks + depth - 1, step, 0)

    dkb[...] = collect(dk_own, dk_recv, dk_send, dk_ss, dk_rs, 0, groups)
    dk_save = pltpu.make_async_copy(dkb, dk_out.at[0], out_sem.at[2])
    dk_save.start()

    def settle(c, carry):
        other = remote(place(c, 1 - core), place(c, 1 - core), f_ss.at[c], f_rs.at[c], sibling, f)
        other.wait_recv()
        final_copy(c).wait_send()

        @pl.when(z < depth - 1)
        def _():
            right_copy(c).wait_send()

        @pl.when(z > 0)
        def _():
            left_copy(c).wait_send()

        return carry

    lax.fori_loop(0, chunks, settle, 0)
    w_save = pltpu.make_async_copy(wfin, w_out, out_sem.at[3])
    w_save.start()
    for d in range(1, BACK + 1):
        @pl.when(s + d < n_s)
        def _():
            v_copy(d).wait_send()
            for i in range(groups):
                k_copy(d, i).wait_send()

        @pl.when(s >= d)
        def _():
            for i in range(groups):
                back_copy(dv_send, dv_recv, dv_ss, dv_rs, d, i).wait_send()
                back_copy(dk_send, dk_recv, dk_ss, dk_rs, d, i).wait_send()
    for j in range(1, n_f):
        x_copy(j).wait_send()
        for h in range(HALVES):
            vg_copy(h, j).wait_send()
    for h in range(HALVES):
        pair_copy(h).wait_send()
    dq_copy.wait()
    vg_save.wait()
    dk_save.wait()
    w_save.wait()


def shards(n_s, n_f, layer_inputs, queries, key_states, value_states, output_gradient, doc_blocks):
    rows = queries.shape[1]
    kvw = key_states.shape[2]
    groups = kvw // HEAD_SIZE
    heads = queries.shape[2] // kvw
    width = layer_inputs.shape[2] // n_f
    chunks = HALVES * SUB
    half_cols = kvw // HALVES
    half_rows = width // 2
    sub_rows = half_rows // SUB
    keys = (BACK + 1) * rows
    V = pltpu.VMEM
    D = pltpu.SemaphoreType.DMA
    scratch = [
        V((rows, queries.shape[2]), BF16),
        V((rows, queries.shape[2]), BF16),
        V((BACK + 1, rows, kvw), BF16),
        V((BACK + 1, rows, kvw), BF16),
        V((n_f, rows, width), BF16),
        V((groups, heads // PAIR, keys, PAIR * rows), F32),
        V((keys, PAIR * rows), F32),
        V((rows, queries.shape[2]), BF16),
        V((rows, kvw), F32),
        V((BACK, rows, kvw), BF16),
        V((BACK, rows, kvw), BF16),
        V((rows, kvw), F32),
        V((BACK, rows, kvw), BF16),
        V((BACK, rows, kvw), BF16),
        V((rows, kvw), BF16),
        V((n_f, rows, kvw), BF16),
        V((HALVES, half_rows, half_cols), F32),
        V((HALVES, half_rows, half_cols), BF16),
        V((HALVES, half_rows, half_cols), BF16),
        V((chunks, sub_rows, half_cols), BF16),
        V((chunks, sub_rows, half_cols), BF16),
        V((chunks, sub_rows, half_cols), BF16),
        V((chunks, sub_rows, half_cols), BF16),
        V((width, kvw), BF16),
        D((5,)), D((4,)),
        D((BACK, groups)), D((BACK, groups)), D((BACK,)), D((BACK,)), D((n_f,)), D((n_f,)),
        D((BACK, groups)), D((BACK, groups)), D((BACK, groups)), D((BACK, groups)),
        D((HALVES, n_f)), D((HALVES, n_f)), D((HALVES,)), D((HALVES,)),
        D((chunks,)), D((chunks,)), D((chunks,)), D((chunks,)), D((chunks,)), D((chunks,)),
    ]
    anywhere = pl.BlockSpec(memory_space=pl.ANY)
    out_shape = [
        jax.ShapeDtypeStruct(queries.shape, BF16),
        jax.ShapeDtypeStruct(key_states.shape, BF16),
        jax.ShapeDtypeStruct(key_states.shape, BF16),
        jax.ShapeDtypeStruct((width, kvw), BF16),
    ]
    return tuple(
        pl.pallas_call(
            functools.partial(kernel, n_s, n_f, groups, heads),
            out_shape=out_shape,
            in_specs=[pl.BlockSpec(memory_space=pltpu.SMEM)] + [anywhere] * 5,
            out_specs=[anywhere] * 4,
            scratch_shapes=scratch,
            compiler_params=pltpu.CompilerParams(collective_id=0, has_side_effects=True),
        )(doc_blocks, layer_inputs, queries, key_states, value_states, output_gradient)
    )


def solution(mesh):
    sizes = dict(mesh.shape)
    return jax.shard_map(
        functools.partial(shards, sizes["seq"], sizes["fsdp"]),
        mesh=mesh,
        in_specs=(P("fsdp", "seq", None),) * 5 + (P("fsdp", None),),
        out_specs=(P("fsdp", "seq", None),) * 3 + (P("fsdp", None),),
        check_vma=False,
    )
```

time: 171 us -> 66.3 us (0.39)
  waiting for transfers between devices: 96.5 us -> 0 us
  Pallas kernels: 0 us -> 60.5 us
  matrix products: 20.8 us -> 0 us
  starting transfers between devices: 17.7 us -> 0 us
  between operations: 14.6 us -> 0.66 us
  local copies, waits for them, and re-layouts: 14.5 us -> 4.97 us
  other arithmetic: 6.15 us -> 0 us
    pallas_call x0 -> x1, Pallas kernels: none -> 60.5 us  [shards(): pl.pallas_call(functools.partial(kernel, n_s, n_f, groups, heads), out_sh...]
    psum x1 -> x0, waiting for transfers between devices: 51.2 us -> none  [shards(): weight_total = lax.psum(weight_share, 'seq').astype(jnp.float32)]
    reduce_scatter x1 -> x0, waiting for transfers between devices: 27.5 us -> none  [shards(): lax.psum_scatter(lax.dot_general(local_inputs, value_grad, (((0,), (0,)),...]
    ppermute x8 -> x0, waiting for transfers between devices: 17.8 us -> none  [passed_along(): return lax.ppermute(x, axis, pairs)]
    ppermute x8 -> x0, starting transfers between devices: 17.6 us -> none  [passed_along(): return lax.ppermute(x, axis, pairs)]
    dot_general x17 -> x0, matrix products: 13.7 us -> none  [the longest x4 3.6 us: group_grads(): jnp.einsum('hrk,rhd->kd', score_gradient, q_group, preferred_element_type...]
    unnamed x50 -> x10, local copies, waits for them, and re-layouts: 14.5 us -> 4.97 us
    sub x4 -> x0, matrix products: 7.15 us -> none  [group_grads(): exps = jnp.exp(scores - row_max)]
  transfers between devices with their start and end apart: 10 -> 0, of which waited for: 6 -> 0; matrix products, arithmetic and copies ran while one was open for 11% -> 0% of each run, Pallas kernels for 0% -> 0%
where the time goes in v1:
time: 66.3 us; the launch traced here: 66.1 us
  Pallas kernels  60.5 us (91%)
  local copies, waits for them, and re-layouts  4.97 us (7%)
    pallas_call x1, Pallas kernels, shards(): pl.pallas_call(functools.partial(kernel, n_s, n_f, groups, heads), out_sh...  60.5 us
    unnamed x10, local copies, waits for them, and re-layouts  4.97 us

profile of v1, /device:TPU:0, one launch (start us, length us, event | category | flops | bytes accessed | tf_op | source)
XLA Modules:
  0.0 66.1 jit_solution(10982059610793127958)
XLA Ops:
  0.6 60.5 %shard_map.93 = (bf16[1,128,4096]{2,1,0:T(8,128)(2,1)}, bf16[1,128,512]{2,1,0:T(8,128)(2,1)}, bf16[1,128,512]{2,1,0:T(8,128)(2,1)}, bf16[1024,512]{1,0:T(8,128)(2,1)}) custom-call(s32[1,4]{1,0:T(1,128)} %doc_ref.1, bf16[1,128,4096]{2,1,0:T(8,128)(2,1)} %x_hbm.1, bf16[1,128,4096]{2,1,0:T(8,128)(2,1)} %q_hbm.1, bf16[1,128,512]{2,1,0:T(8,128)(2,1)} %k_hbm.1, ...), custom_call_target="tpu_custom_call" | custom-call | tf_op jit(solution)/shard_map/pallas_call | solution.py:459
  61.2 0.0 copy-start.2
  61.2 0.0 copy-start
  61.2 2.4 %copy.14 = bf16[1,128,4096]{2,1,0:T(8,128)(2,1)} copy(bf16[1,128,4096]{2,1,0:T(8,128)(2,1)} %get-tuple-element.8) | data formatting | bytes 2097152
  63.6 0.0 copy-done.2
  63.6 0.0 copy-start.1
  63.6 0.7 copy.15
  64.2 0.3 copy-done.1
  64.5 0.7 copy.16
  65.2 0.0 copy-done
  65.2 1.0 %copy.17 = bf16[1024,512]{1,0:T(8,128)(2,1)} copy(bf16[1024,512]{1,0:T(8,128)(2,1)S(1)} %copy-done) | data formatting | bytes 2097152
Async XLA Ops:
  61.2 2.4 %copy-start.2 = (bf16[1,128,512]{2,1,0:T(8,128)(2,1)S(1)}, bf16[1,128,512]{2,1,0:T(8,128)(2,1)}, u32[]{:S(2)}) copy-start(bf16[1,128,512]{2,1,0:T(8,128)(2,1)} %get-tuple-element.9) | copy-start | bytes 393220
  61.2 4.0 %copy-start = (bf16[1024,512]{1,0:T(8,128)(2,1)S(1)}, bf16[1024,512]{1,0:T(8,128)(2,1)}, u32[]{:S(2)}) copy-start(bf16[1024,512]{1,0:T(8,128)(2,1)} %get-tuple-element.11) | copy-start | bytes 3145732
  63.6 1.0 %copy-start.1 = (bf16[1,128,512]{2,1,0:T(8,128)(2,1)S(1)}, bf16[1,128,512]{2,1,0:T(8,128)(2,1)}, u32[]{:S(2)}) copy-start(bf16[1,128,512]{2,1,0:T(8,128)(2,1)} %get-tuple-element.10) | copy-start | bytes 393220

commit v2 on v1

--- a/solution.py
+++ b/solution.py
@@ -14,6 +14,7 @@
 PAIR = 2
 HALVES = 2
 SUB = 4
+SLACK = 3
 MESH = pl.DeviceIdType.MESH
 F32 = jnp.float32
 BF16 = jnp.bfloat16
@@ -321,9 +322,9 @@
     token_count = n_f * n_s * rows
 
     def step(t, carry):
-        to_right = t - z
-        to_left = t - (depth - 1 - z)
-        done = t - jnp.maximum(z, depth - 1 - z)
+        to_right = t - SLACK * z
+        to_left = t - SLACK * (depth - 1 - z)
+        done = t - SLACK * jnp.maximum(z, depth - 1 - z)
 
         def inside(c):
             return jnp.logical_and(c >= 0, c < chunks)
@@ -356,7 +357,7 @@
 
         return carry
 
-    lax.fori_loop(0, chunks + depth - 1, step, 0)
+    lax.fori_loop(0, chunks + SLACK * (depth - 1), step, 0)
 
     dkb[...] = collect(dk_own, dk_recv, dk_send, dk_ss, dk_rs, 0, groups)
     dk_save = pltpu.make_async_copy(dkb, dk_out.at[0], out_sem.at[2])
@@ -402,6 +403,22 @@
     vg_save.wait()
     dk_save.wait()
     w_save.wait()
+
+
+def settle_outputs(*refs):
+    sources, outs, held = refs[:4], refs[4:8], refs[8:12]
+    in_sem, out_sem = refs[12:]
+    loads, saves = [], []
+    for i in range(4):
+        loads.append(pltpu.make_async_copy(sources[i], held[i], in_sem.at[i]))
+        saves.append(pltpu.make_async_copy(held[i], outs[i], out_sem.at[i]))
+    for load in loads:
+        load.start()
+    for load, save in zip(loads, saves):
+        load.wait()
+        save.start()
+    for save in saves:
+        save.wait()
 
 
 def shards(n_s, n_f, layer_inputs, queries, key_states, value_states, output_gradient, doc_blocks):
@@ -455,7 +472,7 @@
         jax.ShapeDtypeStruct(key_states.shape, BF16),
         jax.ShapeDtypeStruct((width, kvw), BF16),
     ]
-    return tuple(
+    made = (
         pl.pallas_call(
             functools.partial(kernel, n_s, n_f, groups, heads),
             out_shape=out_shape,
@@ -465,6 +482,15 @@
             compiler_params=pltpu.CompilerParams(collective_id=0, has_side_effects=True),
         )(doc_blocks, layer_inputs, queries, key_states, value_states, output_gradient)
     )
+    return tuple(
+        pl.pallas_call(
+            settle_outputs,
+            out_shape=out_shape,
+            in_specs=[anywhere] * 4,
+            out_specs=[anywhere] * 4,
+            scratch_shapes=[V(o.shape, BF16) for o in out_shape] + [D((4,)), D((4,))],
+        )(*made)
+    )
 
 
 def solution(mesh):

time: 66.3 us -> 53.6 us (0.81)
  Pallas kernels: 60.5 us -> 52.8 us
  local copies, waits for them, and re-layouts: 4.97 us -> 0 us
    pallas_call x1, Pallas kernels: 60.5 us -> 50.1 us  [shards(): pl.pallas_call(functools.partial(kernel, n_s, n_f, groups, heads), out_sh...]
    unnamed x10 -> x0, local copies, waits for them, and re-layouts: 4.97 us -> none
    pallas_call x0 -> x1, Pallas kernels: none -> 2.7 us  [shards(): pl.pallas_call(settle_outputs, out_shape=out_shape, in_specs=[anywhere] *...]
where the time goes in v2:
time: 53.6 us; the launch traced here: 53.5 us
  Pallas kernels  52.8 us (99%)
  between operations  0.64 us (1%)
    pallas_call x1, Pallas kernels, shards(): pl.pallas_call(functools.partial(kernel, n_s, n_f, groups, heads), out_sh...  50.1 us
    pallas_call x1, Pallas kernels, shards(): pl.pallas_call(settle_outputs, out_shape=out_shape, in_specs=[anywhere] *...  2.7 us

profile of v2, /device:TPU:0, one launch (start us, length us, event | category | flops | bytes accessed | tf_op | source)
XLA Modules:
  0.0 53.5 jit_solution(11969238072261934062)
XLA Ops:
  0.6 50.1 %shard_map.93 = (bf16[1,128,4096]{2,1,0:T(8,128)(2,1)}, bf16[1,128,512]{2,1,0:T(8,128)(2,1)}, bf16[1,128,512]{2,1,0:T(8,128)(2,1)}, bf16[1024,512]{1,0:T(8,128)(2,1)}) custom-call(s32[1,4]{1,0:T(1,128)} %doc_ref.1, bf16[1,128,4096]{2,1,0:T(8,128)(2,1)} %x_hbm.1, bf16[1,128,4096]{2,1,0:T(8,128)(2,1)} %q_hbm.1, bf16[1,128,512]{2,1,0:T(8,128)(2,1)} %k_hbm.1, ...), custom_call_target="tpu_custom_call" | custom-call | tf_op jit(solution)/shard_map/pallas_call | solution.py:476
  50.8 2.7 %shard_map.94 = (bf16[1,128,4096]{2,1,0:T(8,128)(2,1)}, bf16[1,128,512]{2,1,0:T(8,128)(2,1)}, bf16[1,128,512]{2,1,0:T(8,128)(2,1)}, bf16[1024,512]{1,0:T(8,128)(2,1)}) custom-call(bf16[1,128,4096]{2,1,0:T(8,128)(2,1)} %get-tuple-element.8.refs_0_, bf16[1,128,512]{2,1,0:T(8,128)(2,1)} %get-tuple-element.9.refs_1_, ...), custom_call_target="tpu_custom_call" | custom-call | tf_op jit(solution)/shard_map/pallas_call | solution.py:486

commit v3 on v2

--- a/solution.py
+++ b/solution.py
@@ -284,9 +284,9 @@
 
     lax.fori_loop(0, 1, second_pass, 0)
     value_half(0)
-    lax.fori_loop(1, 3, second_pass, 0) if groups > 3 else None
+    lax.fori_loop(1, 2, second_pass, 0)
     value_half(1)
-    lax.fori_loop(3 if groups > 3 else 1, groups, second_pass, 0)
+    lax.fori_loop(2, groups, second_pass, 0)
     dq_copy = pltpu.make_async_copy(dq, dq_out.at[0], out_sem.at[0])
     dq_copy.start()
     vg_save = pltpu.make_async_copy(vgb.at[f], vg_out.at[0], out_sem.at[1])
@@ -296,9 +296,6 @@
         x_copy(j).wait_recv()
     for h in range(HALVES):
         weight_half(h)
-    for h in range(HALVES):
-        pair_copy(h).wait_recv()
-        w_own[h] = w_own[h] + pair_recv[h].astype(F32)
 
     def right_copy(c):
         return remote(right_send.at[c], left_recv.at[c], r_ss.at[c], r_rs.at[c], s + 2, f)
@@ -357,7 +354,11 @@
 
         return carry
 
-    lax.fori_loop(0, chunks + SLACK * (depth - 1), step, 0)
+    for h in range(HALVES):
+        pair_copy(h).wait_recv()
+        w_own[h] = w_own[h] + pair_recv[h].astype(F32)
+        last = (h + 1) * SUB if h < HALVES - 1 else chunks + SLACK * (depth - 1)
+        lax.fori_loop(h * SUB, last, step, 0)
 
     dkb[...] = collect(dk_own, dk_recv, dk_send, dk_ss, dk_rs, 0, groups)
     dk_save = pltpu.make_async_copy(dkb, dk_out.at[0], out_sem.at[2])

time: 53.6 us -> 52.4 us (0.978)
  Pallas kernels: 52.8 us -> 51.6 us
    pallas_call x1, Pallas kernels: 50.1 us -> 48.9 us  [shards(): pl.pallas_call(functools.partial(kernel, n_s, n_f, groups, heads), out_sh...]
where the time goes in v3:
time: 52.4 us; the launch traced here: 52.2 us
  Pallas kernels  51.6 us (98%)
  between operations  0.64 us (1%)
    pallas_call x1, Pallas kernels, shards(): pl.pallas_call(functools.partial(kernel, n_s, n_f, groups, heads), out_sh...  48.9 us
    pallas_call x1, Pallas kernels, shards(): pl.pallas_call(settle_outputs, out_shape=out_shape, in_specs=[anywhere] *...  2.7 us

profile of v3, /device:TPU:0, one launch (start us, length us, event | category | flops | bytes accessed | tf_op | source)
XLA Modules:
  0.0 52.2 jit_solution(18388500847229833822)
XLA Ops:
  0.6 48.9 %shard_map.93 = (bf16[1,128,4096]{2,1,0:T(8,128)(2,1)}, bf16[1,128,512]{2,1,0:T(8,128)(2,1)}, bf16[1,128,512]{2,1,0:T(8,128)(2,1)}, bf16[1024,512]{1,0:T(8,128)(2,1)}) custom-call(s32[1,4]{1,0:T(1,128)} %doc_ref.1, bf16[1,128,4096]{2,1,0:T(8,128)(2,1)} %x_hbm.1, bf16[1,128,4096]{2,1,0:T(8,128)(2,1)} %q_hbm.1, bf16[1,128,512]{2,1,0:T(8,128)(2,1)} %k_hbm.1, ...), custom_call_target="tpu_custom_call" | custom-call | tf_op jit(solution)/shard_map/pallas_call | solution.py:477
  49.5 2.7 %shard_map.94 = (bf16[1,128,4096]{2,1,0:T(8,128)(2,1)}, bf16[1,128,512]{2,1,0:T(8,128)(2,1)}, bf16[1,128,512]{2,1,0:T(8,128)(2,1)}, bf16[1024,512]{1,0:T(8,128)(2,1)}) custom-call(bf16[1,128,4096]{2,1,0:T(8,128)(2,1)} %get-tuple-element.8.refs_0_, bf16[1,128,512]{2,1,0:T(8,128)(2,1)} %get-tuple-element.9.refs_1_, ...), custom_call_target="tpu_custom_call" | custom-call | tf_op jit(solution)/shard_map/pallas_call | solution.py:487
